TPU v7x, 32 devices: a whole 2x2x4 slice. The times are simulated.
32 devices in a mesh: fsdp: 2 (over x), ctx: 4 (over y, core), tp: 4 (over z).
Axes of the slice: x: 2, y: 2, z: 4, core: 2. Of those that a mesh axis runs over, the one named last changes fastest.
Arguments:
- inputs: bfloat16 [4, 1024, 2048], P('fsdp', 'ctx'), may hold values from -6 to 6
- prefix: int32 [4], P('fsdp'), may hold values from 102 to 512, as said below
- expert_ids: int32 [4, 1024, 8], P('fsdp', 'ctx'), may hold values from 0 to 15, all different within a row
- norm_gains: bfloat16 [4, 2048], P(None, ('fsdp', 'ctx')), may hold values from 0.5 to 1.5
- qkv_weight: bfloat16 [3, 2048, 2048], P(None, ('fsdp', 'ctx'), 'tp'), may hold values from -0.125 to 0.125
- out_weight: bfloat16 [2048, 2048], P(('fsdp', 'ctx'), 'tp'), may hold values from -1 to 1
- router_weight: bfloat16 [2048, 16], P(('fsdp', 'ctx')), may hold values from -0.0625 to 0.0625
- gate_up_weight: bfloat16 [16, 2, 2048, 1024], P(None, None, ('fsdp', 'ctx'), 'tp'), may hold values from -0.125 to 0.125
- down_weight: bfloat16 [16, 2048, 1024], P(None, ('fsdp', 'ctx'), 'tp'), may hold values from -1.5 to 1.5
- cotangent: bfloat16 [4, 1024, 2048], P('fsdp', 'ctx'), may hold values from -6 to 6
Outputs:
- outputs: bfloat16 [4, 1024, 2048], P('fsdp', 'ctx')
- grad_inputs: bfloat16 [4, 1024, 2048], P('fsdp', 'ctx')
- grad_norm_gains: float32 [4, 2048], P(None, ('fsdp', 'ctx'))
- grad_qkv_weight: float32 [3, 2048, 2048], P(None, ('fsdp', 'ctx'), 'tp')
- grad_out_weight: float32 [2048, 2048], P(('fsdp', 'ctx'), 'tp')
- grad_router_weight: float32 [2048, 16], P(('fsdp', 'ctx'))
- grad_gate_up_weight: float32 [16, 2, 2048, 1024], P(None, None, ('fsdp', 'ctx'), 'tp')
- grad_down_weight: float32 [16, 2048, 1024], P(None, ('fsdp', 'ctx'), 'tp')
Inputs may be any that keep to these rules, and one draw needn't show every extreme that they name: `expert_ids`: each token names 8 different experts. Some sequence has the shortest and some the longest allowed prefix.
All inputs are finite; a program needn't handle non-finite values.
Results may differ from a plain program's by a relative error of at most 0.017.
Values may be sent and summed in bfloat16 or wider, within the bound.
No kernel may reach another device: no remote copies, remote signals or barrier semaphores. Data moves between devices by JAX's collectives and lax.ppermute only.
A program may use at most 384 MiB of HBM per device.

v0:
```python
import jax
import jax.numpy as jnp
from jax import lax
from jax.sharding import PartitionSpec as P

HEAD_DIM = 128
EPSILON = 1e-05
THETA = 10000.0


def rotary_tables(positions, head_width):
    halves = jnp.arange(0, head_width, 2).astype(jnp.float32) / head_width
    inverse = 1.0 / THETA**halves
    angles = positions.astype(jnp.float32)[:, None] * inverse[None, :]
    return (jnp.cos(angles), jnp.sin(angles))


def rotate(values, cosine, sine):
    half = values.shape[-1] // 2
    first = values[..., :half]
    second = values[..., half:]
    cosine = cosine[:, None, :]
    sine = sine[:, None, :]
    return jnp.concatenate([first * cosine - second * sine, second * cosine + first * sine], -1)


def unrotate(grads, cosine, sine):
    half = grads.shape[-1] // 2
    first = grads[..., :half]
    second = grads[..., half:]
    cosine = cosine[:, None, :]
    sine = sine[:, None, :]
    return jnp.concatenate([first * cosine + second * sine, second * cosine - first * sine], -1)


def contract_rows(left, right):
    return lax.dot_general(
        left, right, (((0,), (0,)), ((), ())), preferred_element_type=jnp.float32
    )


def contract_last(left, right):
    return lax.dot_general(
        left, right, (((1,), (1,)), ((), ())), preferred_element_type=jnp.float32
    )


def body(
    inputs,
    prefix,
    expert_ids,
    norm_gains,
    qkv_weight,
    out_weight,
    router_weight,
    gate_up_weight,
    down_weight,
    cotangent,
):
    sequences, local_len, width = inputs.shape
    tokens = sequences * local_len
    full_len = local_len * lax.axis_size("ctx")
    gains_low, qkv_full, out_full = (
        lax.all_gather(norm_gains, ("fsdp", "ctx"), axis=1, tiled=True),
        lax.all_gather(qkv_weight, ("fsdp", "ctx"), axis=1, tiled=True),
        lax.all_gather(out_weight, ("fsdp", "ctx"), axis=0, tiled=True),
    )
    gains = gains_low.astype(jnp.float32)
    local_width = qkv_full.shape[2]
    head_width = HEAD_DIM
    local_heads = local_width // head_width
    head_scale = head_width ** (-0.5)
    column_start = lax.axis_index("tp") * local_width
    query_gain = lax.dynamic_slice_in_dim(gains[2], column_start, local_width)
    key_gain = lax.dynamic_slice_in_dim(gains[3], column_start, local_width)
    residual = inputs.reshape(tokens, width).astype(jnp.float32)
    scale_one = lax.rsqrt(jnp.mean(residual * residual, -1, keepdims=True) + EPSILON)
    normal_one = residual * scale_one
    normed_one = (normal_one * gains[0]).astype(jnp.bfloat16)
    projected = jnp.einsum("td,cde->cte", normed_one, qkv_full, preferred_element_type=jnp.float32)
    query_raw = projected[0]
    key_raw = projected[1]
    value_raw = projected[2]
    query_squares, key_squares = lax.psum(
        (jnp.sum(query_raw * query_raw, -1), jnp.sum(key_raw * key_raw, -1)), "tp"
    )
    query_scale = lax.rsqrt(query_squares / width + EPSILON)[:, None]
    key_scale = lax.rsqrt(key_squares / width + EPSILON)[:, None]
    query_hat = query_raw * query_scale
    key_hat = key_raw * key_scale
    positions = lax.axis_index("ctx") * local_len + jnp.arange(local_len, dtype=jnp.int32)
    cosine, sine = rotary_tables(positions, head_width)
    head_shape = (sequences, local_len, local_heads, head_width)
    queries = rotate((query_hat * query_gain).reshape(head_shape), cosine, sine).astype(
        jnp.bfloat16
    )
    keys_local = rotate((key_hat * key_gain).reshape(head_shape), cosine, sine).astype(jnp.bfloat16)
    values_local = value_raw.reshape(head_shape).astype(jnp.bfloat16)
    all_keys, all_values = (
        lax.all_gather(keys_local, "ctx", axis=1, tiled=True),
        lax.all_gather(values_local, "ctx", axis=1, tiled=True),
    )
    key_places = jnp.arange(full_len, dtype=jnp.int32)
    visible = (key_places[None, None, :] <= positions[None, :, None]) | (
        key_places[None, None, :] < prefix[:, None, None]
    )
    visible = visible[:, None]
    scores = (
        jnp.einsum("sqhd,skhd->shqk", queries, all_keys, preferred_element_type=jnp.float32)
        * head_scale
    )
    masked = jnp.where(visible, scores, -1e30)
    maxima = jnp.max(masked, -1, keepdims=True)
    expo = jnp.exp(masked - maxima)
    totals = jnp.sum(expo, -1, keepdims=True)
    probs = expo / totals
    log_total = maxima + jnp.log(totals)
    heads_out = jnp.einsum(
        "shqk,skhd->sqhd",
        probs.astype(jnp.bfloat16),
        all_values,
        preferred_element_type=jnp.float32,
    )
    heads_out = heads_out.astype(jnp.bfloat16).reshape(tokens, local_width)
    attn_total = lax.psum(contract_last(heads_out, out_full), "tp")
    mid = residual + attn_total
    scale_two = lax.rsqrt(jnp.mean(mid * mid, -1, keepdims=True) + EPSILON)
    normal_two = mid * scale_two
    normed_two = (normal_two * gains[1]).astype(jnp.bfloat16)
    gate_up_full, down_full, router_full = (
        lax.all_gather(gate_up_weight, ("fsdp", "ctx"), axis=2, tiled=True),
        lax.all_gather(down_weight, ("fsdp", "ctx"), axis=1, tiled=True),
        lax.all_gather(router_weight, ("fsdp", "ctx"), axis=0, tiled=True),
    )
    expert_count = router_full.shape[1]
    logits = jnp.dot(normed_two, router_full, preferred_element_type=jnp.float32)
    router_probs = jax.nn.softmax(logits, -1)
    chosen = jnp.sum(
        (
            expert_ids.reshape(tokens, -1)[:, :, None]
            == jnp.arange(expert_count, dtype=jnp.int32)[None, None, :]
        ).astype(jnp.float32),
        1,
    )
    gates = router_probs * chosen

    def expert_forward(carry, entries):
        pair_weights, down_one, gate_one = entries
        activations = jnp.einsum(
            "td,cdf->ctf", normed_two, pair_weights, preferred_element_type=jnp.float32
        )
        hidden = (gate_one[:, None] * jax.nn.silu(activations[0]) * activations[1]).astype(
            jnp.bfloat16
        )
        return (carry + contract_last(hidden, down_one), activations)

    moe_part, kept_activations = lax.scan(
        expert_forward, jnp.zeros((tokens, width), jnp.float32), (gate_up_full, down_full, gates.T)
    )
    moe_total = lax.psum(moe_part.astype(jnp.bfloat16), "tp").astype(jnp.float32)
    outputs = (mid + moe_total).astype(jnp.bfloat16).reshape(inputs.shape)
    grad_out = cotangent.reshape(tokens, width)
    grad_float = grad_out.astype(jnp.float32)
    gate_up_back, down_back, router_back = (
        lax.all_gather(gate_up_weight, ("fsdp", "ctx"), axis=2, tiled=True),
        lax.all_gather(down_weight, ("fsdp", "ctx"), axis=1, tiled=True),
        lax.all_gather(router_weight, ("fsdp", "ctx"), axis=0, tiled=True),
    )

    def expert_backward(carry, entries):
        pair_weights, down_one, gate_one, activations = entries
        grad_hidden = jnp.dot(grad_out, down_one, preferred_element_type=jnp.float32)
        sigma = jax.nn.sigmoid(activations[0])
        swish = jax.nn.silu(activations[0])
        hidden = (gate_one[:, None] * swish * activations[1]).astype(jnp.bfloat16)
        grad_down = contract_rows(grad_out, hidden)
        grad_gate = jnp.sum(grad_hidden * swish * activations[1], -1)
        grad_inner = grad_hidden * gate_one[:, None]
        grad_act_gate = grad_inner * activations[1] * sigma * (1.0 + activations[0] * (1.0 - sigma))
        grad_act_up = grad_inner * swish
        grad_acts = jnp.stack([grad_act_gate, grad_act_up]).astype(jnp.bfloat16)
        grad_pair = jnp.einsum(
            "td,ctf->cdf", normed_two, grad_acts, preferred_element_type=jnp.float32
        )
        carry = carry + jnp.einsum(
            "ctf,cdf->td", grad_acts, pair_weights, preferred_element_type=jnp.float32
        )
        return (carry, (grad_pair, grad_down, grad_gate))

    back_inputs = (gate_up_back, down_back, gates.T, kept_activations)
    zero_rows = jnp.zeros((tokens, width), jnp.float32)
    expert_part, (grad_gate_up, grad_down_all, grad_gates) = lax.scan(
        expert_backward, zero_rows, back_inputs
    )
    expert_grad_norm, gate_grads = lax.psum((expert_part, grad_gates.T), "tp")
    masked_grads = gate_grads * chosen
    grad_logits = (
        router_probs * (masked_grads - jnp.sum(router_probs * masked_grads, -1, keepdims=True))
    ).astype(jnp.bfloat16)
    grad_router = contract_rows(normed_two, grad_logits)
    grad_normed_two = expert_grad_norm + contract_last(grad_logits, router_back)
    owned_gate_up, owned_down, owned_router = (
        lax.psum_scatter(grad_gate_up, ("fsdp", "ctx"), scatter_dimension=2, tiled=True),
        lax.psum_scatter(grad_down_all, ("fsdp", "ctx"), scatter_dimension=1, tiled=True),
        lax.psum_scatter(grad_router, ("fsdp", "ctx"), scatter_dimension=0, tiled=True),
    )
    weighted_two = grad_normed_two * gains[1]
    grad_mid = grad_float + scale_two * (
        weighted_two - normal_two * jnp.mean(weighted_two * normal_two, -1, keepdims=True)
    )
    gain_two_grad = jnp.sum(grad_normed_two * normal_two, 0)
    grad_mid_low = grad_mid.astype(jnp.bfloat16)
    grad_out_weight = contract_rows(grad_mid_low, heads_out)
    grad_heads = (
        jnp.dot(grad_mid_low, out_full, preferred_element_type=jnp.float32)
        .astype(jnp.bfloat16)
        .reshape(head_shape)
    )
    scores_again = (
        jnp.einsum("sqhd,skhd->shqk", queries, all_keys, preferred_element_type=jnp.float32)
        * head_scale
    )
    probs_again = jnp.exp(jnp.where(visible, scores_again, -1e30) - log_total)
    grad_probs = jnp.einsum(
        "sqhd,skhd->shqk", grad_heads, all_values, preferred_element_type=jnp.float32
    )
    inner_sums = jnp.sum(probs_again * grad_probs, -1, keepdims=True)
    grad_scores = (probs_again * (grad_probs - inner_sums)).astype(jnp.bfloat16)
    grad_queries = (
        jnp.einsum("shqk,skhd->sqhd", grad_scores, all_keys, preferred_element_type=jnp.float32)
        * head_scale
    )
    grad_keys_all = (
        jnp.einsum("shqk,sqhd->skhd", grad_scores, queries, preferred_element_type=jnp.float32)
        * head_scale
    )
    grad_values_all = jnp.einsum(
        "shqk,sqhd->skhd",
        probs_again.astype(jnp.bfloat16),
        grad_heads,
        preferred_element_type=jnp.float32,
    )
    grad_keys, grad_values = (
        lax.psum_scatter(grad_keys_all, "ctx", scatter_dimension=1, tiled=True),
        lax.psum_scatter(grad_values_all, "ctx", scatter_dimension=1, tiled=True),
    )
    grad_query_hat = unrotate(grad_queries, cosine, sine).reshape(tokens, local_width)
    grad_key_hat = unrotate(grad_keys, cosine, sine).reshape(tokens, local_width)
    weighted_query = grad_query_hat * query_gain
    weighted_key = grad_key_hat * key_gain
    query_inner, key_inner = lax.psum(
        (jnp.sum(weighted_query * query_hat, -1), jnp.sum(weighted_key * key_hat, -1)), "tp"
    )
    grad_query_raw = (
        query_scale * (weighted_query - query_hat * (query_inner / width)[:, None])
    ).astype(jnp.bfloat16)
    grad_key_raw = (key_scale * (weighted_key - key_hat * (key_inner / width)[:, None])).astype(
        jnp.bfloat16
    )
    grad_value_raw = grad_values.reshape(tokens, local_width).astype(jnp.bfloat16)
    grad_projected = jnp.stack([grad_query_raw, grad_key_raw, grad_value_raw])
    grad_qkv = jnp.einsum(
        "td,cte->cde", normed_one, grad_projected, preferred_element_type=jnp.float32
    )
    grad_normed_part = jnp.einsum(
        "cte,cde->td", grad_projected, qkv_full, preferred_element_type=jnp.float32
    )
    local_gain_grads = jnp.stack(
        [jnp.sum(grad_query_hat * query_hat, 0), jnp.sum(grad_key_hat * key_hat, 0)]
    )
    placed_gains = lax.dynamic_update_slice_in_dim(
        jnp.zeros((2, width), jnp.float32), local_gain_grads, column_start, 1
    )
    grad_normed_one, qk_gain_grads = lax.psum((grad_normed_part, placed_gains), "tp")
    weighted_one = grad_normed_one * gains[0]
    grad_input = grad_mid + scale_one * (
        weighted_one - normal_one * jnp.mean(weighted_one * normal_one, -1, keepdims=True)
    )
    gain_one_grad = jnp.sum(grad_normed_one * normal_one, 0)
    grad_gains = jnp.stack([gain_one_grad, gain_two_grad, qk_gain_grads[0], qk_gain_grads[1]])
    owned_gains, owned_qkv, owned_out = (
        lax.psum_scatter(grad_gains, ("fsdp", "ctx"), scatter_dimension=1, tiled=True),
        lax.psum_scatter(grad_qkv, ("fsdp", "ctx"), scatter_dimension=1, tiled=True),
        lax.psum_scatter(grad_out_weight, ("fsdp", "ctx"), scatter_dimension=0, tiled=True),
    )
    return (
        outputs,
        grad_input.astype(jnp.bfloat16).reshape(inputs.shape),
        owned_gains,
        owned_qkv,
        owned_out,
        owned_router,
        owned_gate_up,
        owned_down,
    )


def solution(mesh):
    return jax.shard_map(
        body,
        mesh=mesh,
        in_specs=(
            P("fsdp", "ctx", None),
            P("fsdp"),
            P("fsdp", "ctx", None),
            P(None, ("fsdp", "ctx")),
            P(None, ("fsdp", "ctx"), "tp"),
            P(("fsdp", "ctx"), "tp"),
            P(("fsdp", "ctx"), None),
            P(None, None, ("fsdp", "ctx"), "tp"),
            P(None, ("fsdp", "ctx"), "tp"),
            P("fsdp", "ctx", None),
        ),
        out_specs=(
            P("fsdp", "ctx", None),
            P("fsdp", "ctx", None),
            P(None, ("fsdp", "ctx")),
            P(None, ("fsdp", "ctx"), "tp"),
            P(("fsdp", "ctx"), "tp"),
            P(("fsdp", "ctx"), None),
            P(None, None, ("fsdp", "ctx"), "tp"),
            P(None, ("fsdp", "ctx"), "tp"),
        ),
        check_vma=False,
    )
```

profile of v0, /device:TPU:0, one launch (start us, length us, event | category | flops | bytes accessed | tf_op | source)
XLA Modules:
  0.0 2617.0 jit_solution(943007271589671076)
XLA Ops:
  11.9 10.4 all_gather.27
  24.7 35.1 %all-gather.7.cloned.1.call-done = bf16[3,2048,512]{1,2,0:T(8,128)(2,1)} async-done(((bf16[3,256,512]{1,2,0:T(8,128)(2,1)}), bf16[3,2048,512]{1,2,0:T(8,128)(2,1)}) %all-gather.7.cloned.1.call-update) | async-done | bytes 6291472 | tf_op jit(solution)/shard_map/all_gather | solution.py:65
  59.9 6.2 fusion.52
  69.0 11.7 all-reduce.1
  101.0 11.4 all-gather.11.cloned.1.call-done
  121.4 16.0 all-gather.9.cloned.1.call-done
  143.6 23.5 all-gather.13.cloned.1.call-done
  173.5 9.2 all_gather.32
  182.7 144.4 %all-reduce.7.cloned.1.call-done = f32[512,2048]{1,0:T(8,128)} async-done(((f32[512,2048]{1,0:T(8,128)}), f32[512,2048]{1,0:T(8,128)}) %all-reduce.7.cloned.1.call-update) | async-done | bytes 4194320 | tf_op jit(solution)/shard_map/psum | solution.py:125
  332.0 86.0 %all-gather.17.cloned.1.call-done = bf16[16,2048,256]{2,1,0:T(8,128)(2,1)} async-done(((bf16[16,256,256]{2,1,0:T(8,128)(2,1)}), bf16[16,2048,256]{2,1,0:T(8,128)(2,1)}) %all-gather.17.cloned.1.call-update) | async-done | bytes 16777232 | tf_op jit(solution)/shard_map/all_gather | solution.py:132
  418.0 162.9 %all-gather.15.cloned.1.call-done = bf16[16,2,2048,256]{3,2,1,0:T(8,128)(2,1)} async-done(((bf16[16,2,256,256]{3,2,1,0:T(8,128)(2,1)}), bf16[16,2,2048,256]{3,2,1,0:T(8,128)(2,1)}) %all-gather.15.cloned.1.call-update) | async-done | bytes 33554448 | tf_op jit(solution)/shard_map/all_gather | solution.py:131
  580.9 145.9 %while.30 = (s32[]{:T(128)}, f32[512,2048]{1,0:T(8,128)}, f32[16,2,512,256]{2,3,1,0:T(8,128)}, f32[16,512]{1,0:T(8,128)S(1)}, bf16[16,2,2048,256]{3,2,1,0:T(8,12...) while((s32[]{:T(128)}, f32[512,2048]{1,0:T(8,128)}, ...), condition=%wide.region_13.14_spmd.clone, body=%wide.region_12.13_spmd.clone.sunk | while | flops 1613627392 | bytes 50338988 | solution.py:157
  726.8 503.8 %while.31 = (s32[]{:T(128)}, f32[512,2048]{1,0:T(8,128)}, f32[16,2,2048,256]{3,2,1,0:T(8,128)}, f32[16,2048,256]{2,1,0:T(8,128)}, f32[16,512]{1,0:T(8,128)S(1)},...) while((s32[]{:T(128)}, f32[512,2048]{1,0:T(8,128)}, ...), condition=%wide.region_17.18_spmd.clone, body=%wide.region_15.17_spmd.clone.sunk | while | flops 3226992128 | bytes 86523664 | solution.py:192
  767.0 6.2 bitcast_add_fusion.4
  1234.6 20.3 psum.75
  1255.0 131.8 %all-reduce.11.cloned.1.call-done = f32[512,2048]{1,0:T(8,128)} async-done(((f32[512,2048]{1,0:T(8,128)}), f32[512,2048]{1,0:T(8,128)}) %all-reduce.11.cloned.1.call-update) | async-done | bytes 4194320 | tf_op jit(solution)/shard_map/psum | solution.py:195
  1386.7 6.7 multiply_reduce_fusion.2
  1393.4 81.8 %all-reduce.9.cloned.1.call-done = bf16[512,2048]{1,0:T(8,128)(2,1)} async-done(((bf16[512,2048]{1,0:T(8,128)(2,1)}), bf16[512,2048]{1,0:T(8,128)(2,1)}) %all-reduce.9.cloned.1.call-update) | async-done | bytes 2097168 | tf_op jit(solution)/shard_map/psum | solution.py:160
  1475.2 6.7 multiply_add_fusion
  1485.6 7.0 fusion.46
  1514.6 21.7 reduce-scatter.13.cloned.1.call-done
  1541.1 42.3 %reduce-scatter.11.cloned.1.call-done = f32[2,256,4,128]{3,1,2,0:T(8,128)} async-done(((f32[2,1024,4,128]{3,1,2,0:T(8,128)}), f32[2,256,4,128]{3,1,2,0:T(8,128)}) %reduce-scatter.11.cloned.1.call-update) | async-done | bytes 1048592 | tf_op jit(solution)/shard_map/reduce_scatter | solution.py:244
  1601.3 19.0 all-reduce
  1623.6 7.8 convolution_bitcast_fusion.4
  1631.5 152.3 %all-reduce.13.cloned.1.call-done = f32[512,2048]{1,0:T(8,128)} async-done(((f32[512,2048]{1,0:T(8,128)}), f32[512,2048]{1,0:T(8,128)}) %all-reduce.13.cloned.1.call-update) | async-done | bytes 4194320 | tf_op jit(solution)/shard_map/psum | solution.py:274
  1789.7 9.8 convolution_bitcast_fusion.3
  1814.3 10.1 reduce-scatter.25.cloned.1.call-done
  1826.0 94.2 %reduce-scatter.15.cloned.1.call-done = f32[3,256,512]{1,2,0:T(8,128)} async-done(((f32[3,2048,512]{1,2,0:T(8,128)}), f32[3,256,512]{1,2,0:T(8,128)}) %reduce-scatter.15.cloned.1.call-update) | async-done | bytes 1572880 | tf_op jit(solution)/shard_map/reduce_scatter | solution.py:283
  1923.2 33.8 %reduce-scatter.19.cloned.1.call-done = f32[256,16]{0,1:T(8,128)} async-done(((f32[2048,16]{0,1:T(8,128)}), f32[256,16]{0,1:T(8,128)}) %reduce-scatter.19.cloned.1.call-update) | async-done | bytes 16400 | tf_op jit(solution)/shard_map/reduce_scatter | solution.py:205
  1957.0 55.5 %reduce-scatter.17.cloned.1.call-done = f32[256,512]{1,0:T(8,128)} async-done(((f32[2048,512]{1,0:T(8,128)}), f32[256,512]{1,0:T(8,128)}) %reduce-scatter.17.cloned.1.call-update) | async-done | bytes 524304 | tf_op jit(solution)/shard_map/reduce_scatter | solution.py:284
  2012.5 209.3 %reduce-scatter.23.cloned.1.call-done = f32[16,256,256]{2,1,0:T(8,128)} async-done(((f32[16,2048,256]{2,1,0:T(8,128)}), f32[16,256,256]{2,1,0:T(8,128)}) %reduce-scatter.23.cloned.1.call-update) | async-done | bytes 4194320 | tf_op jit(solution)/shard_map/reduce_scatter | solution.py:204
  2221.8 388.2 %reduce-scatter.21.cloned.1.call-done = f32[16,2,256,256]{3,2,1,0:T(8,128)} async-done(((f32[16,2,2048,256]{3,2,1,0:T(8,128)}), f32[16,2,256,256]{3,2,1,0:T(8,128)}) %reduce-scatter.21.cloned.1.call-update) | async-done | bytes 8388624 | tf_op jit(solution)/shard_map/reduce_scatter | solution.py:203
  (564 shorter events, 779.8 us)
Async XLA Ops:
  7.2 52.7 %all-gather.7.cloned.1.call-start = ((), (), s32[]{:S(2)}) async-start(), calls=%async_computation.8 | async-start | bytes 7077888 | tf_op jit(solution)/shard_map/all_gather | solution.py:65
  9.7 102.7 %all-gather.11.cloned.1.call-start = ((), (), s32[]{:S(2)}) async-start(), calls=%async_computation.10 | async-start | bytes 2621440 | tf_op jit(solution)/shard_map/all_gather | solution.py:100
  11.8 54.3 %copy-start.30 = (f32[1,2,2,128]{3,1,2,0:T(2,128)}, f32[1,2,2,128]{3,1,2,0:T(2,128)S(1)}, u32[]{:S(2)}) copy-start(f32[1,2,2,128]{3,1,2,0:T(2,128)S(1)} %copy.139) | copy-start | bytes 6148
  22.3 37.6 %copy-start.28 = (f32[1,2048]{1,0:T(1,128)}, f32[1,2048]{1,0:T(1,128)S(1)}, u32[]{:S(2)}) copy-start(f32[1,2048]{1,0:T(1,128)S(1)} %get-tuple-element.315) | copy-start | bytes 24580
  22.3 66.6 %copy-start.38 = (f32[1,512]{1,0:T(1,128)}, f32[1,512]{1,0:T(1,128)S(1)}, u32[]{:S(2)}) copy-start(f32[1,512]{1,0:T(1,128)S(1)} %get-tuple-element.326) | copy-start | bytes 6148
  22.3 68.0 %copy-start.36 = (f32[1,512]{1,0:T(1,128)}, f32[1,512]{1,0:T(1,128)S(1)}, u32[]{:S(2)}) copy-start(f32[1,512]{1,0:T(1,128)S(1)} %get-tuple-element.325) | copy-start | bytes 6148
  22.9 67.7 %copy-start.19 = (f32[256,64]{1,0:T(8,128)}, f32[256,64]{1,0:T(8,128)S(1)}, u32[]{:S(2)}) copy-start(f32[256,64]{1,0:T(8,128)S(1)} %get-tuple-element.316) | copy-start | bytes 196612
  22.9 67.7 %copy-start.21 = (f32[256,64]{1,0:T(8,128)}, f32[256,64]{1,0:T(8,128)S(1)}, u32[]{:S(2)}) copy-start(f32[256,64]{1,0:T(8,128)S(1)} %get-tuple-element.317) | copy-start | bytes 196612
  91.3 24.9 copy-start.14
  92.4 45.0 %all-gather.9.cloned.1.call-start = ((), (), s32[]{:S(2)}) async-start(), calls=%async_computation.9 | async-start | bytes 2621440 | tf_op jit(solution)/shard_map/all_gather | solution.py:101
  98.5 68.6 %all-gather.13.cloned.1.call-start = ((), (), s32[]{:S(2)}) async-start(), calls=%async_computation.11 | async-start | bytes 2359296 | tf_op jit(solution)/shard_map/all_gather | solution.py:66
  99.1 228.1 %all-reduce.7.cloned.1.call-start = ((), (), s32[]{:S(2)}) async-start(), calls=%async_computation.12 | async-start | bytes 8388608 | tf_op jit(solution)/shard_map/psum | solution.py:125
  143.6 28.5 %copy-start.12 = (bf16[2,256,4,128]{3,2,1,0:T(4,128)(2,1)}, bf16[2,256,4,128]{3,2,1,0:T(4,128)(2,1)S(1)}, u32[]{:S(2)}) copy-start(bf16[2,256,4,128]{3,2,1,0:T(4,128)(2,1)S(1)} %copy.90) | copy-start | bytes 1572868
  172.1 245.9 %all-gather.17.cloned.1.call-start = ((), (), s32[]{:S(2)}) async-start(), calls=%async_computation.14 | async-start | bytes 18874368 | tf_op jit(solution)/shard_map/all_gather | solution.py:132
  172.6 408.2 %all-gather.15.cloned.1.call-start = ((), (), s32[]{:S(2)}) async-start(), calls=%async_computation.13 | async-start | bytes 37748736 | tf_op jit(solution)/shard_map/all_gather | solution.py:131
  173.4 1213.3 %all-reduce.11.cloned.1.call-start = ((), (), s32[]{:S(2)}) async-start(), calls=%async_computation.16 | async-start | bytes 8388608 | tf_op jit(solution)/shard_map/psum | solution.py:195
  1230.6 244.6 %all-reduce.9.cloned.1.call-start = ((), (), s32[]{:S(2)}) async-start(), calls=%async_computation.15 | async-start | bytes 4194304 | tf_op jit(solution)/shard_map/psum | solution.py:160
  1234.5 301.7 %reduce-scatter.13.cloned.1.call-start = ((), (), s32[]{:S(2)}) async-start(), calls=%async_computation.18 | async-start | bytes 5242880 | tf_op jit(solution)/shard_map/reduce_scatter | solution.py:245
  1492.6 90.7 %reduce-scatter.11.cloned.1.call-start = ((), (), s32[]{:S(2)}) async-start(), calls=%async_computation.17 | async-start | bytes 5242880 | tf_op jit(solution)/shard_map/reduce_scatter | solution.py:244
  1509.8 73.5 %copy-start.20 = (f32[256,64]{1,0:T(8,128)S(1)}, f32[256,64]{1,0:T(8,128)}, u32[]{:S(2)}) copy-start(f32[256,64]{1,0:T(8,128)} %copy-done.19) | copy-start | bytes 196612
  1509.8 73.5 %copy-start.22 = (f32[256,64]{1,0:T(8,128)S(1)}, f32[256,64]{1,0:T(8,128)}, u32[]{:S(2)}) copy-start(f32[256,64]{1,0:T(8,128)} %copy-done.21) | copy-start | bytes 196612
  1509.8 274.0 %all-reduce.13.cloned.1.call-start = ((), (), s32[]{:S(2)}) async-start(), calls=%async_computation.19 | async-start | bytes 8388608 | tf_op jit(solution)/shard_map/psum | solution.py:274
  1631.4 152.4 %copy-start.29 = (f32[1,2048]{1,0:T(1,128)S(1)}, f32[1,2048]{1,0:T(1,128)}, u32[]{:S(2)}) copy-start(f32[1,2048]{1,0:T(1,128)} %copy-done.28) | copy-start | bytes 24580
  1631.4 152.4 %copy-start.31 = (f32[1,2,2,128]{3,1,2,0:T(2,128)S(1)}, f32[1,2,2,128]{3,1,2,0:T(2,128)}, u32[]{:S(2)}) copy-start(f32[1,2,2,128]{3,1,2,0:T(2,128)} %copy-done.30) | copy-start | bytes 6148
  1631.4 158.3 %copy-start.24 = (bf16[1,512,512]{1,2,0:T(8,128)(2,1)S(1)}, bf16[1,512,512]{1,2,0:T(8,128)(2,1)}, u32[]{:S(2)}) copy-start(bf16[1,512,512]{1,2,0:T(8,128)(2,1)} %copy-done.23) | copy-start | bytes 1572868
  1631.4 158.3 %copy-start.26 = (bf16[1,512,512]{1,2,0:T(8,128)(2,1)S(1)}, bf16[1,512,512]{1,2,0:T(8,128)(2,1)}, u32[]{:S(2)}) copy-start(bf16[1,512,512]{1,2,0:T(8,128)(2,1)} %copy-done.25) | copy-start | bytes 1572868
  1631.5 193.0 %reduce-scatter.25.cloned.1.call-start = ((), (), s32[]{:S(2)}) async-start(), calls=%async_computation.25 | async-start | bytes 1179648
  1789.2 131.0 %reduce-scatter.15.cloned.1.call-start = ((), (), s32[]{:S(2)}) async-start(), calls=%async_computation.20 | async-start | bytes 14155776 | tf_op jit(solution)/shard_map/reduce_scatter | solution.py:283
  1799.5 157.5 %reduce-scatter.19.cloned.1.call-start = ((), (), s32[]{:S(2)}) async-start(), calls=%async_computation.22 | async-start | bytes 147456 | tf_op jit(solution)/shard_map/reduce_scatter | solution.py:205
  1800.6 211.9 %reduce-scatter.17.cloned.1.call-start = ((), (), s32[]{:S(2)}) async-start(), calls=%async_computation.21 | async-start | bytes 4718592 | tf_op jit(solution)/shard_map/reduce_scatter | solution.py:284
  1806.2 415.6 %reduce-scatter.23.cloned.1.call-start = ((), (), s32[]{:S(2)}) async-start(), calls=%async_computation.24 | async-start | bytes 37748736 | tf_op jit(solution)/shard_map/reduce_scatter | solution.py:204
  1806.8 803.2 %reduce-scatter.21.cloned.1.call-start = ((), (), s32[]{:S(2)}) async-start(), calls=%async_computation.23 | async-start | bytes 75497472 | tf_op jit(solution)/shard_map/reduce_scatter | solution.py:203
  (105 other events, 403.3 us)
Sparse Core Ops, SparseCore 0:
  10.5 49.3 all-gather.6
  92.6 19.8 all-gather.10
  114.6 22.8 all-gather.8
  139.2 27.8 all-gather.12
  172.2 154.9 all-reduce.6
  329.1 88.8 all-gather.16
  420.0 160.7 all-gather.14
  1230.7 155.9 all-reduce.10
  1389.7 85.5 all-reduce.8
  1492.8 43.4 reduce-scatter.12
  1538.8 44.5 reduce-scatter.10
  1631.6 152.2 all-reduce.12
  1789.3 35.0 reduce-scatter.24
  1827.8 92.3 reduce-scatter.14
  1923.6 33.3 reduce-scatter.18
  1961.1 51.3 reduce-scatter.16
  2016.5 205.2 reduce-scatter.22
  2226.2 383.7 reduce-scatter.20
where the time goes:
time: 2630 us; the launch traced here: 2620 us
  waiting for transfers between devices  1700 us (65%)
  matrix products  489 us (19%)
  local copies, waits for them, and re-layouts  282 us (11%)
  blocking collectives  70.5 us (3%)
  other arithmetic  54.7 us (2%)
    reduce_scatter x1, waiting for transfers between devices, body(): lax.psum_scatter(grad_gate_up, ('fsdp', 'ctx'), scatter_dimension=2, tile...  388 us
    reduce_scatter x1, waiting for transfers between devices, body(): lax.psum_scatter(grad_down_all, ('fsdp', 'ctx'), scatter_dimension=1, til...  209 us
    dynamic_update_slice x80, local copies, waits for them, and re-layouts, body(): lax.scan(expert_backward, zero_rows, back_inputs)  176 us
    all_gather x1, waiting for transfers between devices, body(): lax.all_gather(gate_up_weight, ('fsdp', 'ctx'), axis=2, tiled=True)  163 us
    psum x1, waiting for transfers between devices, body(): lax.psum((grad_normed_part, placed_gains), 'tp')  152 us
    psum x1, waiting for transfers between devices, body(): attn_total = lax.psum(contract_last(heads_out, out_full), 'tp')  144 us
    psum x1, waiting for transfers between devices, body(): expert_grad_norm, gate_grads = lax.psum((expert_part, grad_gates.T), 'tp')  132 us
    dot_general x16, matrix products, expert_backward(): jnp.einsum('ctf,cdf->td', grad_acts, pair_weights, preferred_element_type...  97.3 us
  transfers between devices with their start and end apart: 18, of which 18 were waited for; matrix products, arithmetic and copies ran while one was open for 3% of the time, Pallas kernels for 0%

commit v1 on v0

--- a/solution.py
+++ b/solution.py
@@ -2,10 +2,40 @@
 import jax.numpy as jnp
 from jax import lax
 from jax.sharding import PartitionSpec as P
+from jax.lax import axis_index, axis_size, ppermute
 
 HEAD_DIM = 128
 EPSILON = 1e-05
 THETA = 10000.0
+
+
+def divide_the_spot(view):
+    bus_axis = ("fsdp", "ctx")
+    local_now, part_now, last = (axis_size(bus_axis), axis_index(bus_axis), view.shape[1])
+    copies = []
+    for w, kk in enumerate(view.shape):
+        copies.append(kk * local_now if w == 1 else kk)
+    arr_out = lax.dynamic_update_slice_in_dim(
+        jnp.zeros(copies, view.dtype), view, part_now * last, axis=1
+    )
+    shaped = aux = view
+    for t in range(1, local_now // 2 + 1):
+        pages = []
+        for w in range(local_now):
+            pages.append((w, (w + 1) % local_now))
+        shaped = ppermute(shaped, bus_axis, pages)
+        arr_out = lax.dynamic_update_slice_in_dim(
+            arr_out, shaped, (part_now - t) % local_now * last, axis=1
+        )
+        if 2 * t < local_now:
+            parts_seen = []
+            for w in range(local_now):
+                parts_seen.append((w, (w - 1) % local_now))
+            aux = ppermute(aux, bus_axis, parts_seen)
+            arr_out = lax.dynamic_update_slice_in_dim(
+                arr_out, aux, (part_now + t) % local_now * last, axis=1
+            )
+    return arr_out
 
 
 def rotary_tables(positions, head_width):
@@ -129,7 +159,7 @@
     normed_two = (normal_two * gains[1]).astype(jnp.bfloat16)
     gate_up_full, down_full, router_full = (
         lax.all_gather(gate_up_weight, ("fsdp", "ctx"), axis=2, tiled=True),
-        lax.all_gather(down_weight, ("fsdp", "ctx"), axis=1, tiled=True),
+        divide_the_spot(down_weight),
         lax.all_gather(router_weight, ("fsdp", "ctx"), axis=0, tiled=True),
     )
     expert_count = router_full.shape[1]

time: 2630 us -> 2540 us (0.966)
  waiting for transfers between devices: 1700 us -> 1460 us
  starting transfers between devices: 1.97 us -> 109 us
  local copies, waits for them, and re-layouts: 282 us -> 309 us
    psum x1, waiting for transfers between devices: 144 us -> 0.01 us  [body(): attn_total = lax.psum(contract_last(heads_out, out_full), 'tp')]
    ppermute x0 -> x7, starting transfers between devices: none -> 107 us  [the longest x4 105 us: divide_the_spot(): shaped = ppermute(shaped, bus_axis, pages)]
    all_gather x1, waiting for transfers between devices: 86 us -> 0.01 us  [body(): lax.all_gather(down_weight, ('fsdp', 'ctx'), axis=1, tiled=True)]
    all_gather x1, waiting for transfers between devices: 163 us -> 113 us  [body(): lax.all_gather(gate_up_weight, ('fsdp', 'ctx'), axis=2, tiled=True)]
    ppermute x0 -> x7, waiting for transfers between devices: none -> 33.8 us  [the longest x4 33.8 us: divide_the_spot(): shaped = ppermute(shaped, bus_axis, pages)]
  transfers between devices with their start and end apart: 18 -> 25, of which waited for: 18 -> 19; matrix products, arithmetic and copies ran while one was open for 3% -> 9% of each run, Pallas kernels for 0% -> 0%
where the time goes in v1:
time: 2540 us; the launch traced here: 2530 us
  waiting for transfers between devices  1460 us (57%)
  matrix products  490 us (19%)
  local copies, waits for them, and re-layouts  309 us (12%)
  starting transfers between devices  109 us (4%)
  blocking collectives  92.6 us (4%)
  other arithmetic  54.7 us (2%)
    reduce_scatter x1, waiting for transfers between devices, body(): lax.psum_scatter(grad_gate_up, ('fsdp', 'ctx'), scatter_dimension=2, tile...  388 us
    reduce_scatter x1, waiting for transfers between devices, body(): lax.psum_scatter(grad_down_all, ('fsdp', 'ctx'), scatter_dimension=1, til...  209 us
    dynamic_update_slice x80, local copies, waits for them, and re-layouts, body(): lax.scan(expert_backward, zero_rows, back_inputs)  177 us
    psum x1, waiting for transfers between devices, body(): lax.psum((grad_normed_part, placed_gains), 'tp')  152 us
    psum x1, waiting for transfers between devices, body(): expert_grad_norm, gate_grads = lax.psum((expert_part, grad_gates.T), 'tp')  132 us
    all_gather x1, waiting for transfers between devices, body(): lax.all_gather(gate_up_weight, ('fsdp', 'ctx'), axis=2, tiled=True)  113 us
    ppermute x4, starting transfers between devices, divide_the_spot(): shaped = ppermute(shaped, bus_axis, pages)  105 us
    dot_general x16, matrix products, expert_backward(): jnp.einsum('ctf,cdf->td', grad_acts, pair_weights, preferred_element_type...  96.8 us
  transfers between devices with their start and end apart: 25, of which 19 were waited for; matrix products, arithmetic and copies ran while one was open for 9% of the time, Pallas kernels for 0%

profile of v1, /device:TPU:0, one launch (start us, length us, event | category | flops | bytes accessed | tf_op | source)
XLA Modules:
  0.0 2529.2 jit_solution(1386468456552333079)
XLA Ops:
  11.9 10.4 all_gather.26
  24.7 35.1 %all-gather.7.cloned.1.call-done = bf16[3,2048,512]{1,2,0:T(8,128)(2,1)} async-done(((bf16[3,256,512]{1,2,0:T(8,128)(2,1)}), bf16[3,2048,512]{1,2,0:T(8,128)(2,1)}) %all-gather.7.cloned.1.call-update) | async-done | bytes 6291472 | tf_op jit(solution)/shard_map/all_gather | solution.py:95
  69.1 11.7 all-reduce.1
  100.7 11.8 all-gather.11.cloned.1.call-done
  121.5 16.0 all-gather.9.cloned.1.call-done
  143.6 23.5 all-gather.13.cloned.1.call-done
  176.2 24.0 collective-permute-done
  201.5 20.6 collective-permute-start.2
  228.0 40.3 %collective-permute-start.4 = (bf16[16,256,256]{2,1,0:T(8,128)(2,1)S(1)}, bf16[16,256,256]{2,1,0:T(8,128)(2,1)}, u32[]{:S(2)}, u32[]{:S(2)}) collective-permute-start(bf16[16,256,256]{2,1,0:T(8,128)(2,1)S(1)} %collective-permute-done.2), channel_id=1, source_target_pairs={{0,4},{4,8},{8,12},{12,16},{16,20},{20,24},{24,28},{28,0},{1,5},{5... | collective-permute-start | bytes 6291464 | tf_op jit(solution)/shard_map/ppermute | solution.py:26
  272.3 43.3 %collective-permute-start.6 = (bf16[16,256,256]{2,1,0:T(8,128)(2,1)}, bf16[16,256,256]{2,1,0:T(8,128)(2,1)}, u32[]{:S(2)}, u32[]{:S(2)}) collective-permute-start(bf16[16,256,256]{2,1,0:T(8,128)(2,1)} %collective-permute-done.4), channel_id=1, source_target_pairs={{0,4},{4,8},{8,12},{12,16},{16,20},{20,24},{24,28},{28,0},{1,5},{5... | collective-permute-start | bytes 6291464 | tf_op jit(solution)/shard_map/ppermute | solution.py:26
  315.6 30.8 %all_gather.31 = bf16[2048,16]{0,1:T(8,128)(2,1)S(1)} all-gather(bf16[256,16]{0,1:T(8,128)(2,1)S(1)} %copy-done.48), channel_id=1, replica_groups=mesh['fsdp'=2,'ctx'=4,'tp'=4] {'fsdp','ctx'}, dimensions={0}, use_global_device_ids=true | all-gather | bytes 73728 | tf_op jit(solution)/shard_map/all_gather | solution.py:163
  376.0 113.0 %all-gather.15.cloned.1.call-done = bf16[16,2,2048,256]{3,2,1,0:T(8,128)(2,1)} async-done(((bf16[16,2,256,256]{3,2,1,0:T(8,128)(2,1)}), bf16[16,2,2048,256]{3,2,1,0:T(8,128)(2,1)}) %all-gather.15.cloned.1.call-update) | async-done | bytes 33554448 | tf_op jit(solution)/shard_map/all_gather | solution.py:161
  489.0 147.4 %while.30 = (s32[]{:T(128)}, f32[512,2048]{1,0:T(8,128)}, f32[16,2,512,256]{2,3,1,0:T(8,128)}, f32[16,512]{1,0:T(8,128)S(1)}, bf16[16,2,2048,256]{3,2,1,0:T(8,12...) while((s32[]{:T(128)}, f32[512,2048]{1,0:T(8,128)}, ...), condition=%wide.region_13.14_spmd.clone, body=%wide.region_12.13_spmd.clone.sunk | while | flops 1613627392 | bytes 50338988 | solution.py:187
  636.3 505.4 %while.31 = (s32[]{:T(128)}, f32[512,2048]{1,0:T(8,128)}, f32[16,2,2048,256]{3,2,1,0:T(8,128)}, f32[16,2048,256]{2,1,0:T(8,128)}, f32[16,512]{1,0:T(8,128)S(1)},...) while((s32[]{:T(128)}, f32[512,2048]{1,0:T(8,128)}, ...), condition=%wide.region_17.18_spmd.clone, body=%wide.region_15.17_spmd.clone.sunk | while | flops 3226992128 | bytes 86523664 | solution.py:222
  1146.1 20.8 psum.75
  1167.0 131.9 %all-reduce.11.cloned.1.call-done = f32[512,2048]{1,0:T(8,128)} async-done(((f32[512,2048]{1,0:T(8,128)}), f32[512,2048]{1,0:T(8,128)}) %all-reduce.11.cloned.1.call-update) | async-done | bytes 4194320 | tf_op jit(solution)/shard_map/psum | solution.py:225
  1299.0 6.7 multiply_reduce_fusion.2
  1305.6 81.8 %all-reduce.9.cloned.1.call-done = bf16[512,2048]{1,0:T(8,128)(2,1)} async-done(((bf16[512,2048]{1,0:T(8,128)(2,1)}), bf16[512,2048]{1,0:T(8,128)(2,1)}) %all-reduce.9.cloned.1.call-update) | async-done | bytes 2097168 | tf_op jit(solution)/shard_map/psum | solution.py:190
  1387.5 6.7 multiply_add_fusion
  1397.8 7.0 fusion.46
  1426.7 21.7 reduce-scatter.13.cloned.1.call-done
  1453.3 42.3 %reduce-scatter.11.cloned.1.call-done = f32[2,256,4,128]{3,1,2,0:T(8,128)} async-done(((f32[2,1024,4,128]{3,1,2,0:T(8,128)}), f32[2,256,4,128]{3,1,2,0:T(8,128)}) %reduce-scatter.11.cloned.1.call-update) | async-done | bytes 1048592 | tf_op jit(solution)/shard_map/reduce_scatter | solution.py:274
  1513.6 18.9 all-reduce
  1535.8 7.8 convolution_bitcast_fusion.4
  1543.7 152.4 %all-reduce.13.cloned.1.call-done = f32[512,2048]{1,0:T(8,128)} async-done(((f32[512,2048]{1,0:T(8,128)}), f32[512,2048]{1,0:T(8,128)}) %all-reduce.13.cloned.1.call-update) | async-done | bytes 4194320 | tf_op jit(solution)/shard_map/psum | solution.py:304
  1701.7 9.8 convolution_bitcast_fusion.3
  1726.3 10.3 reduce-scatter.25.cloned.1.call-done
  1738.2 94.2 %reduce-scatter.15.cloned.1.call-done = f32[3,256,512]{1,2,0:T(8,128)} async-done(((f32[3,2048,512]{1,2,0:T(8,128)}), f32[3,256,512]{1,2,0:T(8,128)}) %reduce-scatter.15.cloned.1.call-update) | async-done | bytes 1572880 | tf_op jit(solution)/shard_map/reduce_scatter | solution.py:313
  1835.4 33.8 %reduce-scatter.19.cloned.1.call-done = f32[256,16]{0,1:T(8,128)} async-done(((f32[2048,16]{0,1:T(8,128)}), f32[256,16]{0,1:T(8,128)}) %reduce-scatter.19.cloned.1.call-update) | async-done | bytes 16400 | tf_op jit(solution)/shard_map/reduce_scatter | solution.py:235
  1869.2 55.5 %reduce-scatter.17.cloned.1.call-done = f32[256,512]{1,0:T(8,128)} async-done(((f32[2048,512]{1,0:T(8,128)}), f32[256,512]{1,0:T(8,128)}) %reduce-scatter.17.cloned.1.call-update) | async-done | bytes 524304 | tf_op jit(solution)/shard_map/reduce_scatter | solution.py:314
  1924.7 209.3 %reduce-scatter.23.cloned.1.call-done = f32[16,256,256]{2,1,0:T(8,128)} async-done(((f32[16,2048,256]{2,1,0:T(8,128)}), f32[16,256,256]{2,1,0:T(8,128)}) %reduce-scatter.23.cloned.1.call-update) | async-done | bytes 4194320 | tf_op jit(solution)/shard_map/reduce_scatter | solution.py:234
  2134.0 388.2 %reduce-scatter.21.cloned.1.call-done = f32[16,2,256,256]{3,2,1,0:T(8,128)} async-done(((f32[16,2,2048,256]{3,2,1,0:T(8,128)}), f32[16,2,256,256]{3,2,1,0:T(8,128)}) %reduce-scatter.21.cloned.1.call-update) | async-done | bytes 8388624 | tf_op jit(solution)/shard_map/reduce_scatter | solution.py:233
  (601 shorter events, 833.5 us)
Async XLA Ops:
  7.2 52.7 %all-gather.7.cloned.1.call-start = ((), (), s32[]{:S(2)}) async-start(), calls=%async_computation.8 | async-start | bytes 7077888 | tf_op jit(solution)/shard_map/all_gather | solution.py:95
  9.7 102.8 %all-gather.11.cloned.1.call-start = ((), (), s32[]{:S(2)}) async-start(), calls=%async_computation.10 | async-start | bytes 2621440 | tf_op jit(solution)/shard_map/all_gather | solution.py:130
  92.5 45.0 %all-gather.9.cloned.1.call-start = ((), (), s32[]{:S(2)}) async-start(), calls=%async_computation.9 | async-start | bytes 2621440 | tf_op jit(solution)/shard_map/all_gather | solution.py:131
  98.6 68.6 %all-gather.13.cloned.1.call-start = ((), (), s32[]{:S(2)}) async-start(), calls=%async_computation.11 | async-start | bytes 2359296 | tf_op jit(solution)/shard_map/all_gather | solution.py:96
  99.1 272.0 %all-reduce.7.cloned.1.call-start = ((), (), s32[]{:S(2)}) async-start(), calls=%async_computation.12 | async-start | bytes 8388608 | tf_op jit(solution)/shard_map/psum | solution.py:155
  172.1 143.5 %copy-start.48 = (bf16[256,16]{0,1:T(8,128)(2,1)S(1)}, bf16[256,16]{0,1:T(8,128)(2,1)}, u32[]{:S(2)}) copy-start(bf16[256,16]{0,1:T(8,128)(2,1)} %param.20) | copy-start | bytes 24580
  172.1 174.3 %copy-start.47 = (s32[2,256,8]{1,2,0:T(8,128)S(1)}, s32[2,256,8]{1,2,0:T(8,128)}, u32[]{:S(2)}) copy-start(s32[2,256,8]{1,2,0:T(8,128)} %param.16) | copy-start | bytes 49156
  172.1 316.9 %all-gather.15.cloned.1.call-start = ((), (), s32[]{:S(2)}) async-start(), calls=%async_computation.13 | async-start | bytes 37748736 | tf_op jit(solution)/shard_map/all_gather | solution.py:161
  172.7 463.6 %all-gather.17.cloned.1.call-start = ((), (), s32[]{:S(2)}) async-start(), calls=%async_computation.15 | async-start | bytes 18874368 | tf_op jit(solution)/shard_map/all_gather | solution.py:196
  173.4 1125.5 %all-reduce.11.cloned.1.call-start = ((), (), s32[]{:S(2)}) async-start(), calls=%async_computation.16 | async-start | bytes 8388608 | tf_op jit(solution)/shard_map/psum | solution.py:225
  173.5 26.7 %collective-permute-start = (bf16[16,256,256]{2,1,0:T(8,128)(2,1)}, bf16[16,256,256]{2,1,0:T(8,128)(2,1)S(1)}, u32[]{:S(2)}, u32[]{:S(2)}) collective-permute-start(bf16[16,256,256]{2,1,0:T(8,128)(2,1)} %param.22), channel_id=1, source_target_pairs={{0,4},{4,8},{8,12},{12,16},{16,20},{20,24},{24,28},{28,0},{1,5},{5... | collective-permute-start | bytes 6291464 | tf_op jit(solution)/shard_map/ppermute | solution.py:26
  173.8 48.3 %collective-permute-start.1 = (bf16[16,256,256]{2,1,0:T(8,128)(2,1)}, bf16[16,256,256]{2,1,0:T(8,128)(2,1)S(1)}, u32[]{:S(2)}, u32[]{:S(2)}) collective-permute-start(bf16[16,256,256]{2,1,0:T(8,128)(2,1)} %param.22), channel_id=1, source_target_pairs={{0,28},{4,0},{8,4},{12,8},{16,12},{20,16},{24,20},{28,24},{1,29},{... | collective-permute-start | bytes 6291464 | tf_op jit(solution)/shard_map/ppermute | solution.py:34
  201.5 26.5 %collective-permute-start.2 = (bf16[16,256,256]{2,1,0:T(8,128)(2,1)S(1)}, bf16[16,256,256]{2,1,0:T(8,128)(2,1)S(1)}, u32[]{:S(2)}, u32[]{:S(2)}) collective-permute-start(bf16[16,256,256]{2,1,0:T(8,128)(2,1)S(1)} %collective-permute-done), channel_id=1, source_target_pairs={{0,4},{4,8},{8,12},{12,16},{16,20},{20,24},{24,28},{28,0},{1,5},{5... | collective-permute-start | bytes 6291464 | tf_op jit(solution)/shard_map/ppermute | solution.py:26
  222.1 46.2 %collective-permute-start.3 = (bf16[16,256,256]{2,1,0:T(8,128)(2,1)S(1)}, bf16[16,256,256]{2,1,0:T(8,128)(2,1)}, u32[]{:S(2)}, u32[]{:S(2)}) collective-permute-start(bf16[16,256,256]{2,1,0:T(8,128)(2,1)S(1)} %collective-permute-done.1), channel_id=1, source_target_pairs={{0,28},{4,0},{8,4},{12,8},{16,12},{20,16},{24,20},{28,24},{1,29},{... | collective-permute-start | bytes 6291464 | tf_op jit(solution)/shard_map/ppermute | solution.py:34
  228.0 44.3 %collective-permute-start.4 = (bf16[16,256,256]{2,1,0:T(8,128)(2,1)S(1)}, bf16[16,256,256]{2,1,0:T(8,128)(2,1)}, u32[]{:S(2)}, u32[]{:S(2)}) collective-permute-start(bf16[16,256,256]{2,1,0:T(8,128)(2,1)S(1)} %collective-permute-done.2), channel_id=1, source_target_pairs={{0,4},{4,8},{8,12},{12,16},{16,20},{20,24},{24,28},{28,0},{1,5},{5... | collective-permute-start | bytes 6291464 | tf_op jit(solution)/shard_map/ppermute | solution.py:26
  268.4 96.6 %collective-permute-start.5 = (bf16[16,256,256]{2,1,0:T(8,128)(2,1)}, bf16[16,256,256]{2,1,0:T(8,128)(2,1)}, u32[]{:S(2)}, u32[]{:S(2)}) collective-permute-start(bf16[16,256,256]{2,1,0:T(8,128)(2,1)} %collective-permute-done.3), channel_id=1, source_target_pairs={{0,28},{4,0},{8,4},{12,8},{16,12},{20,16},{24,20},{28,24},{1,29},{... | collective-permute-start | bytes 6291464 | tf_op jit(solution)/shard_map/ppermute | solution.py:34
  272.3 95.8 %collective-permute-start.6 = (bf16[16,256,256]{2,1,0:T(8,128)(2,1)}, bf16[16,256,256]{2,1,0:T(8,128)(2,1)}, u32[]{:S(2)}, u32[]{:S(2)}) collective-permute-start(bf16[16,256,256]{2,1,0:T(8,128)(2,1)} %collective-permute-done.4), channel_id=1, source_target_pairs={{0,4},{4,8},{8,12},{12,16},{16,20},{20,24},{24,28},{28,0},{1,5},{5... | collective-permute-start | bytes 6291464 | tf_op jit(solution)/shard_map/ppermute | solution.py:26
  1141.7 245.7 %all-reduce.9.cloned.1.call-start = ((), (), s32[]{:S(2)}) async-start(), calls=%async_computation.14 | async-start | bytes 4194304 | tf_op jit(solution)/shard_map/psum | solution.py:190
  1145.6 302.8 %reduce-scatter.13.cloned.1.call-start = ((), (), s32[]{:S(2)}) async-start(), calls=%async_computation.18 | async-start | bytes 5242880 | tf_op jit(solution)/shard_map/reduce_scatter | solution.py:275
  1404.8 90.7 %reduce-scatter.11.cloned.1.call-start = ((), (), s32[]{:S(2)}) async-start(), calls=%async_computation.17 | async-start | bytes 5242880 | tf_op jit(solution)/shard_map/reduce_scatter | solution.py:274
  1422.0 73.6 %copy-start.27 = (f32[256,64]{1,0:T(8,128)S(1)}, f32[256,64]{1,0:T(8,128)}, u32[]{:S(2)}) copy-start(f32[256,64]{1,0:T(8,128)} %copy-done.26) | copy-start | bytes 196612
  1422.0 274.0 %all-reduce.13.cloned.1.call-start = ((), (), s32[]{:S(2)}) async-start(), calls=%async_computation.19 | async-start | bytes 8388608 | tf_op jit(solution)/shard_map/psum | solution.py:304
  1543.6 152.5 %copy-start.36 = (f32[1,2048]{1,0:T(1,128)S(1)}, f32[1,2048]{1,0:T(1,128)}, u32[]{:S(2)}) copy-start(f32[1,2048]{1,0:T(1,128)} %copy-done.35) | copy-start | bytes 24580
  1543.6 152.5 %copy-start.38 = (f32[1,2,2,128]{3,1,2,0:T(2,128)S(1)}, f32[1,2,2,128]{3,1,2,0:T(2,128)}, u32[]{:S(2)}) copy-start(f32[1,2,2,128]{3,1,2,0:T(2,128)} %copy-done.37) | copy-start | bytes 6148
  1543.6 158.1 %copy-start.31 = (bf16[1,512,512]{1,2,0:T(8,128)(2,1)S(1)}, bf16[1,512,512]{1,2,0:T(8,128)(2,1)}, u32[]{:S(2)}) copy-start(bf16[1,512,512]{1,2,0:T(8,128)(2,1)} %copy-done.30) | copy-start | bytes 1572868
  1543.6 158.1 %copy-start.33 = (bf16[1,512,512]{1,2,0:T(8,128)(2,1)S(1)}, bf16[1,512,512]{1,2,0:T(8,128)(2,1)}, u32[]{:S(2)}) copy-start(bf16[1,512,512]{1,2,0:T(8,128)(2,1)} %copy-done.32) | copy-start | bytes 1572868
  1543.6 193.0 %reduce-scatter.25.cloned.1.call-start = ((), (), s32[]{:S(2)}) async-start(), calls=%async_computation.25 | async-start | bytes 1179648
  1701.4 131.0 %reduce-scatter.15.cloned.1.call-start = ((), (), s32[]{:S(2)}) async-start(), calls=%async_computation.20 | async-start | bytes 14155776 | tf_op jit(solution)/shard_map/reduce_scatter | solution.py:313
  1711.5 157.7 %reduce-scatter.19.cloned.1.call-start = ((), (), s32[]{:S(2)}) async-start(), calls=%async_computation.22 | async-start | bytes 147456 | tf_op jit(solution)/shard_map/reduce_scatter | solution.py:235
  1712.6 212.1 %reduce-scatter.17.cloned.1.call-start = ((), (), s32[]{:S(2)}) async-start(), calls=%async_computation.21 | async-start | bytes 4718592 | tf_op jit(solution)/shard_map/reduce_scatter | solution.py:314
  1718.2 415.8 %reduce-scatter.23.cloned.1.call-start = ((), (), s32[]{:S(2)}) async-start(), calls=%async_computation.24 | async-start | bytes 37748736 | tf_op jit(solution)/shard_map/reduce_scatter | solution.py:234
  1718.8 803.4 %reduce-scatter.21.cloned.1.call-start = ((), (), s32[]{:S(2)}) async-start(), calls=%async_computation.23 | async-start | bytes 75497472 | tf_op jit(solution)/shard_map/reduce_scatter | solution.py:233
  (119 other events, 943.7 us)
Sparse Core Ops, SparseCore 0:
  10.5 49.3 all-gather.6
  92.6 19.8 all-gather.10
  114.6 22.8 all-gather.8
  139.2 27.8 all-gather.12
  172.2 154.9 all-reduce.6
  329.1 159.7 all-gather.14
  491.0 89.8 all-gather.16
  1141.9 157.0 all-reduce.10
  1301.9 85.5 all-reduce.8
  1405.0 43.4 reduce-scatter.12
  1451.0 44.5 reduce-scatter.10
  1543.7 152.2 all-reduce.12
  1701.5 35.0 reduce-scatter.24
  1740.0 92.3 reduce-scatter.14
  1835.8 33.3 reduce-scatter.18
  1873.3 51.3 reduce-scatter.16
  1928.7 205.2 reduce-scatter.22
  2138.4 383.7 reduce-scatter.20
